TPU v7x, 32 devices: a whole 2x2x4 slice. The times are simulated.
32 devices in a mesh: groups: 2 (over x), mp: 8 (over z, y), row: 2 (over core).
Axes of the slice: x: 2, y: 2, z: 4, core: 2. Of those that a mesh axis runs over, the one named last changes fastest.
Arguments:
- stream: bfloat16 [2, 256, 4096], P(None, ('groups', 'row'), 'mp'), parts along dimension 1, may hold values from -12 to 12
- projected: bfloat16 [2, 256, 2, 8192], P(None, ('groups', 'row'), None, 'mp'), parts along dimension 1, may hold values from -6 to 6
- conv_state: bfloat16 [256, 3, 8192], P(('groups', 'row'), None, 'mp'), parts along dimension 0, may hold values from -6 to 6
- scan_state: float32 [256, 16, 8192], P(('groups', 'row'), None, 'mp'), parts along dimension 0, may hold values from -6 to 6
- conv_weight: float32 [4, 8192], P(None, 'mp'), may hold values from -3 to 3
- conv_bias: float32 [8192], P('mp'), may hold values from -3 to 3
- state_proj: bfloat16 [8192, 288], P('mp'), may hold values from -0.0625 to 0.0625
- step_proj: bfloat16 [256, 8192], P(None, 'mp'), may hold values from -0.375 to 0.375
- step_bias: float32 [8192], P('mp'), may hold values from -3 to 0.5
- decay_log: float32 [16, 8192], P(None, 'mp'), may hold values from -4 to 2
- skip_gain: float32 [8192], P('mp'), may hold values from 0.25 to 1.75
- out_weight: bfloat16 [8192, 4096], P('mp'), may hold values from -0.09375 to 0.09375
- norm_gain: float32 [4096], replicated, may hold values from 0.25 to 1.75
- router: bfloat16 [16, 4096], replicated, may hold values from -0.09375 to 0.09375
- expert_gate: bfloat16 [2, 4096, 12288], P('row', None, 'mp'), may hold values from -0.09375 to 0.09375
- expert_up: bfloat16 [2, 4096, 12288], P('row', None, 'mp'), may hold values from -0.09375 to 0.09375
- expert_down: bfloat16 [2, 12288, 4096], P('row', 'mp'), may hold values from -0.078125 to 0.078125
- expert_ids: int32 [2, 256, 2], P(None, ('groups', 'row')), parts along dimension 1, may hold values from 0 to 15, as said below
Outputs:
- mixed_out: bfloat16 [2, 256, 4096], P(None, ('groups', 'row'), 'mp'), parts along dimension 1
- new_state: float32 [256, 16, 8192], P(('groups', 'row'), None, 'mp'), parts along dimension 0
There are 2 independent parts, one for each index of `groups`. A program takes and returns all parts, laid end to end along the dimension named above; an argument that names none is the same for every part. Nothing has to cross between parts.
Inputs may be any that keep to these rules, and one draw needn't show every extreme that they name: `expert_ids`: A row's two ids differ. In each step, at most 16 of the rows of one device (aligned blocks of 64 rows) choose expert 0, and at most 16 choose expert 1; in every draw some step has exactly 16 such rows for both experts in every block.
All inputs are finite; a program needn't handle non-finite values.
Results may differ from a plain program's by a relative error of at most 0.006.
Values may be sent and summed in bfloat16 or wider, within the bound.
A program may use at most 128 MiB of HBM per device.

v0:
```python
import jax
import jax.numpy as jnp
from jax import lax
from jax.sharding import PartitionSpec as P

CAP = 16


def expert_apply(tokens_in, gate_weight, up_weight, down_weight):
    gate_part = jnp.dot(tokens_in, gate_weight, preferred_element_type=jnp.float32)
    up_part = jnp.dot(tokens_in, up_weight, preferred_element_type=jnp.float32)
    hidden = (jax.nn.silu(gate_part) * up_part).astype(jnp.bfloat16)
    return jnp.dot(hidden, down_weight, preferred_element_type=jnp.float32)


def on_device(
    stream,
    projected,
    conv_state,
    scan_state,
    conv_weight,
    conv_bias,
    state_proj,
    step_proj,
    step_bias,
    decay_log,
    skip_gain,
    out_weight,
    norm_gain,
    router,
    expert_gate,
    expert_up,
    expert_down,
    expert_ids,
):
    step_count, row_count, width_local = stream.shape
    inner_local = projected.shape[3]
    kernel_size = conv_weight.shape[0]
    rank_size = step_proj.shape[0]
    state_size = decay_log.shape[0]
    full_width = out_weight.shape[1]
    flat_rows = step_count * row_count
    inputs = projected[:, :, 0, :]
    gate_side = projected[:, :, 1, :]
    history = jnp.concatenate(
        [conv_state.astype(jnp.float32), jnp.transpose(inputs, (1, 0, 2)).astype(jnp.float32)],
        axis=1,
    )
    conv_list = []
    for step_no in range(step_count):
        window = history[:, step_no : step_no + kernel_size, :]
        conv_list.append(
            jax.nn.silu(jnp.sum(window * conv_weight[None], axis=1) + conv_bias).astype(
                jnp.bfloat16
            )
        )
    convolved = jnp.stack(conv_list)
    local_proj = jnp.dot(
        convolved.reshape(flat_rows, inner_local), state_proj, preferred_element_type=jnp.float32
    )
    projections = lax.psum(local_proj, "mp").reshape(step_count, row_count, -1)
    low_rank = projections[..., :rank_size].astype(jnp.bfloat16)
    input_gain = projections[..., rank_size : rank_size + state_size]
    output_gain = projections[..., rank_size + state_size :]
    timestep = jax.nn.softplus(
        jnp.dot(
            low_rank.reshape(flat_rows, rank_size), step_proj, preferred_element_type=jnp.float32
        ).reshape(step_count, row_count, inner_local)
        + step_bias
    )
    decay_rates = jnp.exp(decay_log)
    carried = scan_state
    outputs = []
    for step_no in range(step_count):
        current = convolved[step_no].astype(jnp.float32)
        delta_now = timestep[step_no]
        decay_now = jnp.exp(-delta_now[:, None, :] * decay_rates[None])
        carried = (
            decay_now * carried
            + (delta_now * current)[:, None, :] * input_gain[step_no][:, :, None]
        )
        readout = jnp.sum(output_gain[step_no][:, :, None] * carried, axis=1) + skip_gain * current
        outputs.append(
            (readout * jax.nn.silu(gate_side[step_no].astype(jnp.float32))).astype(jnp.bfloat16)
        )
    scanned = jnp.stack(outputs).reshape(flat_rows, inner_local)
    partial_value = jnp.dot(scanned, out_weight, preferred_element_type=jnp.float32)
    offset = lax.axis_index("mp") * width_local
    own_part = stream.reshape(flat_rows, width_local).astype(jnp.float32)
    placed = lax.dynamic_update_slice_in_dim(
        partial_value,
        lax.dynamic_slice_in_dim(partial_value, offset, width_local, 1) + own_part,
        offset,
        1,
    )
    after_full = lax.psum(placed, "mp").astype(jnp.bfloat16)
    after_own = lax.dynamic_slice_in_dim(after_full, offset, width_local, 1)
    widened = after_full.astype(jnp.float32)
    normed = (
        widened * lax.rsqrt(jnp.mean(widened * widened, axis=-1, keepdims=True) + 1e-05) * norm_gain
    ).astype(jnp.bfloat16)
    logits = lax.dot_general(
        normed, router, (((1,), (1,)), ((), ())), preferred_element_type=jnp.float32
    )
    picked = expert_ids.reshape(flat_rows, -1)
    expert_total = router.shape[0]
    onehot = picked[:, :, None] == jnp.arange(expert_total)[None, None, :]
    chosen = jnp.sum(jnp.where(onehot, logits[:, None, :], 0.0), axis=2)
    weights = jnp.exp(chosen)
    shares = weights / jnp.sum(weights, axis=1, keepdims=True)
    in_flight = lax.axis_size("row")
    weight_rows = jnp.stack(
        [jnp.sum(jnp.where(picked == expert, shares, 0.0), axis=1) for expert in range(in_flight)],
        axis=1,
    )
    gate_weight = expert_gate[0]
    up_weight = expert_up[0]
    down_weight = expert_down[0]
    routed = jnp.any(picked[:, None, :] == jnp.arange(in_flight)[None, :, None], axis=2)
    position = (
        jnp.cumsum(routed.reshape(step_count, row_count, in_flight).astype(jnp.int32), axis=1) - 1
    ).reshape(flat_rows, in_flight)
    slot_total = step_count * CAP
    slot_index = jnp.arange(slot_total)
    row_step = jnp.arange(flat_rows) // row_count
    matching = (
        jnp.transpose(routed)[:, None, :]
        & (row_step[None, None, :] == (slot_index // CAP)[None, :, None])
        & (jnp.transpose(position)[:, None, :] == (slot_index % CAP)[None, :, None])
    )
    select_half = matching.astype(jnp.bfloat16)
    select_full = matching.astype(jnp.float32)
    outgoing = jnp.einsum(
        "esm,mx->esx", select_half, normed, preferred_element_type=jnp.float32
    ).astype(jnp.bfloat16)
    slot_share = jnp.einsum("esm,me->es", select_full, weight_rows, precision=lax.Precision.HIGHEST)
    arrived = lax.all_to_all(outgoing, "row", split_axis=0, concat_axis=0, tiled=True)
    count_here = arrived.shape[1]
    produced = expert_apply(
        arrived.reshape(-1, full_width), gate_weight, up_weight, down_weight
    ).reshape(in_flight, count_here, full_width)
    returned = lax.all_to_all(
        produced.astype(jnp.bfloat16), "row", split_axis=0, concat_axis=0, tiled=True
    ).astype(produced.dtype)
    combined = jnp.einsum(
        "esm,esx->mx",
        select_full,
        returned * slot_share[:, :, None],
        precision=lax.Precision.HIGHEST,
    )
    combined = lax.psum_scatter(combined, "mp", scatter_dimension=1, tiled=True)
    mixed_out = (
        (after_own.astype(jnp.float32) + combined)
        .astype(jnp.bfloat16)
        .reshape(step_count, row_count, width_local)
    )
    return (mixed_out, carried)


def solution(mesh):
    return jax.shard_map(
        on_device,
        mesh=mesh,
        in_specs=(
            P(None, ("groups", "row"), "mp"),
            P(None, ("groups", "row"), None, "mp"),
            P(("groups", "row"), None, "mp"),
            P(("groups", "row"), None, "mp"),
            P(None, "mp"),
            P("mp"),
            P("mp", None),
            P(None, "mp"),
            P("mp"),
            P(None, "mp"),
            P("mp"),
            P("mp", None),
            P(),
            P(),
            P("row", None, "mp"),
            P("row", None, "mp"),
            P("row", "mp", None),
            P(None, ("groups", "row"), None),
        ),
        out_specs=(P(None, ("groups", "row"), "mp"), P(("groups", "row"), None, "mp")),
        check_vma=False,
    )
```

profile of v0, /device:TPU:0, one launch (start us, length us, event | category | flops | bytes accessed | tf_op | source)
XLA Modules:
  0.0 296.4 jit_solution(5089809884289274848)
XLA Ops:
  7.2 1.2 copy.64
  8.5 1.1 maximum_convert_fusion
  9.6 0.9 fusion.19
  10.6 0.2 multiply_convert_fusion.3
  10.8 1.1 fusion.59
  12.0 0.6 fusion.58
  12.6 0.1 eq.75
  12.7 0.1 copy.51
  12.8 0.1 reduce_window_sum.11
  13.1 72.3 %all-reduce.3.cloned.1.call-done = f32[2,64,288]{2,1,0:T(8,128)} async-done(((f32[2,64,288]{2,1,0:T(8,128)}), f32[2,64,288]{2,1,0:T(8,128)}) %all-reduce.3.cloned.1.call-update) | async-done | bytes 147472 | tf_op jit(solution)/shard_map/psum | solution.py:61
  85.4 1.5 compare_select_fusion
  87.0 0.2 convert_multiply_fusion.5
  87.1 0.9 slice_bitcast_fusion.5
  88.1 7.0 %multiply_reduce_fusion = (f32[64,1024]{1,0:T(8,128)S(1)}, f32[64,16,1024]{2,1,0:T(8,128)}, f32[64,1024]{1,0:T(8,128)S(1)}) fusion(f32[64,16]{1,0:T(8,128)S(1)} %get-tuple-element.17, f32[64,16]{1,0:T(8,128)S(1)} %get-tuple-element.16, f32[64,1024]{1,0:T(8,128)S(1)} %get-tuple-element.10, f32[64,16]{1,0:T(8,128)S(1)} %get-tuple-element.18, ...), kind=kLoop, calls=%fused_computation.9 | loop fusion | flops 12451840 | bytes 10043392 | tf_op jit(solution)/shard_map/reduce_sum | solution.py:82
  95.1 0.2 fusion.40
  95.4 1.3 fusion.60
  96.7 92.4 %all-reduce.4 = bf16[128,4096]{1,0:T(8,128)(2,1)} all-reduce(f32[128,4096]{1,0:T(8,128)S(1)} %fusion.38), channel_id=1, replica_groups=mesh['groups'=2,'mp'=8,'row'=2] {'mp'}, use_global_device_ids=true, to_apply=%region_5.6 | all-reduce | flops 524288 | bytes 3145728 | tf_op jit(solution)/shard_map/psum | solution.py:96
  189.1 1.5 fusion.15
  190.7 1.7 fusion.27
  192.4 0.1 div.112
  192.8 1.9 convolution_convert_fusion
  194.7 0.2 fusion.43
  194.9 4.2 %all_to_all.10 = bf16[2,32,4096]{2,1,0:T(8,128)(2,1)S(1)} all-to-all(bf16[2,32,4096]{2,1,0:T(8,128)(2,1)S(1)} %convolution_convert_fusion), channel_id=1, replica_groups=mesh['groups'=2,'mp'=8,'row'=2] {'row'}, dimensions={0} | all-to-all | bytes 1048576 | tf_op jit(solution)/shard_map/all_to_all | solution.py:137
  199.1 7.0 %fusion.4 = f32[64,1536]{1,0:T(8,128)S(1)} fusion(bf16[64,4096]{1,0:T(8,128)(2,1)S(1)} %bitcast.119, bf16[1,4096,1536]{2,1,0:T(8,128)(2,1)} %param.32), kind=kOutput, calls=%fused_computation.4 | convolution fusion | flops 805306368 | bytes 13500416 | tf_op jit(solution)/shard_map/dot_general | solution.py:10
  206.1 2.3 fusion.12
  208.4 0.1 slice-done.6
  208.5 1.4 slice-done.7
  209.9 2.3 fusion.6
  212.2 4.2 %all_to_all.11 = bf16[2,32,4096]{2,1,0:T(8,128)(2,1)S(1)} all-to-all(bf16[2,32,4096]{2,1,0:T(8,128)(2,1)S(1)} %fusion.6), channel_id=1, replica_groups=mesh['groups'=2,'mp'=8,'row'=2] {'row'}, dimensions={0} | all-to-all | bytes 1048576 | tf_op jit(solution)/shard_map/all_to_all | solution.py:142
  216.4 2.4 convolution_bitcast_fusion
  218.8 69.1 %reduce-scatter.2.cloned.1.call-done = f32[128,512]{1,0:T(8,128)} async-done(((f32[128,4096]{1,0:T(8,128)}), f32[128,512]{1,0:T(8,128)}) %reduce-scatter.2.cloned.1.call-update) | async-done | bytes 262160 | tf_op jit(solution)/shard_map/reduce_scatter | solution.py:151
  287.9 1.7 add_convert_fusion
  (65 shorter events, 0.9 us)
Async XLA Ops:
  7.2 3.6 %copy-start = (bf16[1024,288]{0,1:T(8,128)(2,1)S(1)}, bf16[1024,288]{0,1:T(8,128)(2,1)}, u32[]{:S(2)}) copy-start(bf16[1024,288]{0,1:T(8,128)(2,1)} %param.24) | copy-start | bytes 1769476
  7.2 4.8 %copy-start.2 = (bf16[2,64,2,1024]{3,2,1,0:T(2,128)(2,1)S(1)}, bf16[2,64,2,1024]{3,2,1,0:T(2,128)(2,1)}, u32[]{:S(2)}) copy-start(bf16[2,64,2,1024]{3,2,1,0:T(2,128)(2,1)} %param.19) | copy-start | bytes 1572868
  7.2 3.4 %copy-start.5 = (f32[1024]{0:T(1024)S(1)}, f32[1024]{0:T(1024)}, u32[]{:S(2)}) copy-start(f32[1024]{0:T(1024)} %param.23) | copy-start | bytes 12292
  7.2 78.2 %all-reduce.3.cloned.1.call-start = ((), (), s32[]{:S(2)}) async-start(), calls=%async_computation.3 | async-start | bytes 393216 | tf_op jit(solution)/shard_map/psum | solution.py:61
  8.5 4.1 %copy-start.6 = (s32[2,64,2]{1,2,0:T(2,128)S(1)}, s32[2,64,2]{1,2,0:T(2,128)}, u32[]{:S(2)}) copy-start(s32[2,64,2]{1,2,0:T(2,128)} %param.35) | copy-start | bytes 3076
  8.5 4.5 %copy-start.4 = (f32[16,1024]{1,0:T(8,128)S(1)}, f32[16,1024]{1,0:T(8,128)}, u32[]{:S(2)}) copy-start(f32[16,1024]{1,0:T(8,128)} %param.27) | copy-start | bytes 196612
  8.5 77.0 %copy-start.8 = (bf16[256,1024]{1,0:T(8,128)(2,1)S(1)}, bf16[256,1024]{1,0:T(8,128)(2,1)}, u32[]{:S(2)}) copy-start(bf16[256,1024]{1,0:T(8,128)(2,1)} %param.25) | copy-start | bytes 1572868
  8.5 76.9 %copy-start.11 = (f32[1024]{0:T(1024)S(1)}, f32[1024]{0:T(1024)}, u32[]{:S(2)}) copy-start(f32[1024]{0:T(1024)} %param.26) | copy-start | bytes 12292
  11.9 276.0 %reduce-scatter.2.cloned.1.call-start = ((), (), s32[]{:S(2)}) async-start(), calls=%async_computation.4 | async-start | bytes 2359296 | tf_op jit(solution)/shard_map/reduce_scatter | solution.py:151
  85.4 9.9 %slice-start.3 = ((s8[8388608]{0:T(1024)(128)(4,1)}), s8[4194304]{0:T(1024)(128)(4,1)S(1)}, s32[]{:S(2)}) async-start(s8[8388608]{0:T(1024)(128)(4,1)} %bitcast.115), calls=%async_computation.8 | async-start | bytes 8388608
  88.1 7.0 %copy-start.7 = (f32[1024]{0:T(1024)S(1)}, f32[1024]{0:T(1024)}, u32[]{:S(2)}) copy-start(f32[1024]{0:T(1024)} %param.28) | copy-start | bytes 12292
  88.1 7.3 %slice-start.4 = ((s8[8388608]{0:T(1024)(128)(4,1)}), s8[4194304]{0:T(1024)(128)(4,1)S(1)}, s32[]{:S(2)}) async-start(s8[8388608]{0:T(1024)(128)(4,1)} %bitcast.115), calls=%async_computation.9 | async-start | bytes 8388608
  95.3 1.3 copy-start.3
  96.7 94.0 %copy-start.9 = (bf16[16,4096]{1,0:T(8,128)(2,1)S(1)}, bf16[16,4096]{1,0:T(8,128)(2,1)}, u32[]{:S(2)}) copy-start(bf16[16,4096]{1,0:T(8,128)(2,1)} %param.31) | copy-start | bytes 393220
  96.7 94.0 %copy-start.10 = (f32[4096]{0:T(1024)S(1)}, f32[4096]{0:T(1024)}, u32[]{:S(2)}) copy-start(f32[4096]{0:T(1024)} %param.30) | copy-start | bytes 49156
  192.8 13.3 %slice-start = ((s8[12582912]{0:T(1024)(128)(4,1)}), s8[4194304]{0:T(1024)(128)(4,1)S(1)}, s32[]{:S(2)}) async-start(s8[12582912]{0:T(1024)(128)(4,1)} %bitcast.113), calls=%async_computation.5 | async-start | bytes 8388608
  199.0 7.0 %slice-start.1 = ((s8[12582912]{0:T(1024)(128)(4,1)}), s8[4194304]{0:T(1024)(128)(4,1)S(1)}, s32[]{:S(2)}) async-start(s8[12582912]{0:T(1024)(128)(4,1)} %bitcast.113), calls=%async_computation.6 | async-start | bytes 8388608
  199.1 7.0 %slice-start.2 = ((s8[12582912]{0:T(1024)(128)(4,1)}), s8[4194304]{0:T(1024)(128)(4,1)S(1)}, s32[]{:S(2)}) async-start(s8[12582912]{0:T(1024)(128)(4,1)} %bitcast.113), calls=%async_computation.7 | async-start | bytes 8388608
  199.1 9.3 %slice-start.5 = ((s8[12582912]{0:T(1024)(128)(4,1)}), s8[4194304]{0:T(1024)(128)(4,1)S(1)}, s32[]{:S(2)}) async-start(s8[12582912]{0:T(1024)(128)(4,1)} %bitcast.117), calls=%async_computation.10 | async-start | bytes 8388608
  199.1 9.4 %slice-start.6 = ((s8[12582912]{0:T(1024)(128)(4,1)}), s8[4194304]{0:T(1024)(128)(4,1)S(1)}, s32[]{:S(2)}) async-start(s8[12582912]{0:T(1024)(128)(4,1)} %bitcast.117), calls=%async_computation.11 | async-start | bytes 8388608
  206.1 3.8 %slice-start.7 = ((s8[12582912]{0:T(1024)(128)(4,1)}), s8[4194304]{0:T(1024)(128)(4,1)S(1)}, s32[]{:S(2)}) async-start(s8[12582912]{0:T(1024)(128)(4,1)} %bitcast.117), calls=%async_computation.12 | async-start | bytes 8388608
  209.9 79.7 %copy-start.1 = (bf16[1024,288]{0,1:T(8,128)(2,1)S(1)}, bf16[1024,288]{0,1:T(8,128)(2,1)}, u32[]{:S(2)}) copy-start(bf16[1024,288]{0,1:T(8,128)(2,1)} %param.24) | copy-start | bytes 1769476
Sparse Core Ops, SparseCore 0:
  12.0 73.3 all-reduce.2
  218.9 68.9 reduce-scatter.1
where the time goes:
time: 297 us; the launch traced here: 296 us
  waiting for transfers between devices  141 us (47%)
  blocking collectives  101 us (34%)
  matrix products  21.6 us (7%)
  between operations  14.4 us (5%)
  other arithmetic  13.2 us (4%)
  local copies, waits for them, and re-layouts  4.98 us (2%)
    psum x1, blocking collectives, on_device(): after_full = lax.psum(placed, 'mp').astype(jnp.bfloat16)  92.4 us
    psum x1, waiting for transfers between devices, on_device(): projections = lax.psum(local_proj, 'mp').reshape(step_count, row_count, -1)  72.3 us
    reduce_scatter x1, waiting for transfers between devices, on_device(): combined = lax.psum_scatter(combined, 'mp', scatter_dimension=1, tiled=True)  69.1 us
    reduce_sum x1, other arithmetic, on_device(): jnp.sum(output_gain[step_no][:, :, None] * carried, axis=1)  6.97 us
    dot_general x1, matrix products, expert_apply(): jnp.dot(tokens_in, gate_weight, preferred_element_type=jnp.float32)  6.97 us
  transfers between devices with their start and end apart: 2, of which 2 were waited for; matrix products, arithmetic and copies ran while one was open for 0% of the time, Pallas kernels for 0%

commit v1 on v0

--- a/solution.py
+++ b/solution.py
@@ -58,7 +58,9 @@
     local_proj = jnp.dot(
         convolved.reshape(flat_rows, inner_local), state_proj, preferred_element_type=jnp.float32
     )
-    projections = lax.psum(local_proj, "mp").reshape(step_count, row_count, -1)
+    projections = jnp.sum(lax.all_gather(local_proj, "mp"), axis=0).reshape(
+        step_count, row_count, -1
+    )
     low_rank = projections[..., :rank_size].astype(jnp.bfloat16)
     input_gain = projections[..., rank_size : rank_size + state_size]
     output_gain = projections[..., rank_size + state_size :]

time: 297 us -> 265 us (0.89)
  waiting for transfers between devices: 141 us -> 111 us
    psum x1 -> x0, waiting for transfers between devices: 72.3 us -> none  [on_device(): projections = lax.psum(local_proj, 'mp').reshape(step_count, row_count, -1)]
    all_gather x0 -> x1, waiting for transfers between devices: none -> 42 us  [on_device(): lax.all_gather(local_proj, 'mp')]
where the time goes in v1:
time: 265 us
  waiting for transfers between devices  111 us (42%)
  blocking collectives  99.8 us (38%)
  matrix products  20.5 us (8%)
  between operations  14.4 us (5%)
  other arithmetic  13.7 us (5%)
  local copies, waits for them, and re-layouts  5.78 us (2%)
    psum x1, blocking collectives, on_device(): after_full = lax.psum(placed, 'mp').astype(jnp.bfloat16)  91.5 us
    reduce_scatter x1, waiting for transfers between devices, on_device(): combined = lax.psum_scatter(combined, 'mp', scatter_dimension=1, tiled=True)  68.6 us
    all_gather x1, waiting for transfers between devices, on_device(): lax.all_gather(local_proj, 'mp')  42 us
    reduce_sum x1, other arithmetic, on_device(): jnp.sum(output_gain[step_no][:, :, None] * carried, axis=1)  7.22 us
    dot_general x1, matrix products, expert_apply(): jnp.dot(tokens_in, gate_weight, preferred_element_type=jnp.float32)  6.97 us
  transfers between devices with their start and end apart: 2, of which 2 were waited for; matrix products, arithmetic and copies ran while one was open for 0% of the time, Pallas kernels for 0%

profile of v1, /device:TPU:0, one launch (start us, length us, event | category | flops | bytes accessed | tf_op | source)
XLA Modules:
  0.0 264.9 jit_solution(13403900074671189723)
XLA Ops:
  7.3 1.2 copy.74
  8.5 1.1 maximum_convert_fusion
  9.6 0.9 fusion.19
  10.5 0.2 multiply_convert_fusion.3
  10.8 1.0 fusion.59
  11.9 0.1 copy.60
  12.1 0.1 reduce_window_sum.11
  12.4 0.6 fusion.58
  12.9 42.0 %all-gather.3.cloned.1.call-done = f32[1024,288]{0,1:T(8,128)} async-done(((f32[128,288]{0,1:T(8,128)}), f32[1024,288]{0,1:T(8,128)}) %all-gather.3.cloned.1.call-update) | async-done | bytes 1179664 | tf_op jit(solution)/shard_map/all_gather | solution.py:61
  55.0 1.5 copy.64
  56.5 0.3 bitcast_reduce_fusion
  56.8 0.1 copy.50
  57.0 0.5 compare_select_fusion
  57.5 0.2 convert_multiply_fusion.5
  57.7 7.2 %multiply_reduce_fusion = (f32[64,1024]{1,0:T(8,128)S(1)}, f32[64,16,1024]{2,1,0:T(8,128)}, f32[64,1024]{1,0:T(8,128)S(1)}) fusion(f32[64,16]{1,0:T(8,128)S(1)} %get-tuple-element.17, f32[64,16]{1,0:T(8,128)S(1)} %get-tuple-element.16, f32[64,1024]{1,0:T(8,128)S(1)} %get-tuple-element.10, f32[64,16]{1,0:T(8,128)S(1)} %get-tuple-element.18, ...), kind=kLoop, calls=%fused_computation.9 | loop fusion | flops 12451840 | bytes 10043392 | tf_op jit(solution)/shard_map/reduce_sum | solution.py:84
  64.9 0.2 fusion.40
  65.2 1.3 fusion.60
  66.6 91.5 %all-reduce.1 = bf16[128,4096]{1,0:T(8,128)(2,1)} all-reduce(f32[128,4096]{1,0:T(8,128)S(1)} %fusion.38), channel_id=1, replica_groups=mesh['groups'=2,'mp'=8,'row'=2] {'mp'}, use_global_device_ids=true, to_apply=%region_5.6 | all-reduce | flops 524288 | bytes 3145728 | tf_op jit(solution)/shard_map/psum | solution.py:98
  158.1 1.5 fusion.15
  159.6 1.7 fusion.27
  161.7 1.9 convolution_convert_fusion
  163.6 0.2 fusion.43
  163.8 4.2 %all_to_all.10 = bf16[2,32,4096]{2,1,0:T(8,128)(2,1)S(1)} all-to-all(bf16[2,32,4096]{2,1,0:T(8,128)(2,1)S(1)} %convolution_convert_fusion), channel_id=1, replica_groups=mesh['groups'=2,'mp'=8,'row'=2] {'row'}, dimensions={0} | all-to-all | bytes 1048576 | tf_op jit(solution)/shard_map/all_to_all | solution.py:139
  168.0 7.0 %fusion.4 = f32[64,1536]{1,0:T(8,128)S(1)} fusion(bf16[64,4096]{1,0:T(8,128)(2,1)S(1)} %bitcast.124, bf16[1,4096,1536]{2,1,0:T(8,128)(2,1)} %param.32), kind=kOutput, calls=%fused_computation.4 | convolution fusion | flops 805306368 | bytes 13500416 | tf_op jit(solution)/shard_map/dot_general | solution.py:10
  175.1 2.3 fusion.12
  177.4 0.1 slice-done.6
  177.4 1.4 slice-done.7
  178.9 2.3 fusion.6
  181.2 4.2 %all_to_all.11 = bf16[2,32,4096]{2,1,0:T(8,128)(2,1)S(1)} all-to-all(bf16[2,32,4096]{2,1,0:T(8,128)(2,1)S(1)} %fusion.6), channel_id=1, replica_groups=mesh['groups'=2,'mp'=8,'row'=2] {'row'}, dimensions={0} | all-to-all | bytes 1048576 | tf_op jit(solution)/shard_map/all_to_all | solution.py:144
  185.3 2.4 convolution_bitcast_fusion
  187.8 68.6 %reduce-scatter.2.cloned.1.call-done = f32[128,512]{1,0:T(8,128)} async-done(((f32[128,4096]{1,0:T(8,128)}), f32[128,512]{1,0:T(8,128)}) %reduce-scatter.2.cloned.1.call-update) | async-done | bytes 262160 | tf_op jit(solution)/shard_map/reduce_scatter | solution.py:153
  256.4 1.7 add_convert_fusion
  (68 shorter events, 1.2 us)
Async XLA Ops:
  7.2 3.6 %copy-start = (bf16[1024,288]{0,1:T(8,128)(2,1)S(1)}, bf16[1024,288]{0,1:T(8,128)(2,1)}, u32[]{:S(2)}) copy-start(bf16[1024,288]{0,1:T(8,128)(2,1)} %param.24) | copy-start | bytes 1769476
  7.2 3.4 %copy-start.5 = (f32[1024]{0:T(1024)S(1)}, f32[1024]{0:T(1024)}, u32[]{:S(2)}) copy-start(f32[1024]{0:T(1024)} %param.23) | copy-start | bytes 12292
  7.2 4.6 %copy-start.6 = (s32[2,64,2]{1,2,0:T(2,128)S(1)}, s32[2,64,2]{1,2,0:T(2,128)}, u32[]{:S(2)}) copy-start(s32[2,64,2]{1,2,0:T(2,128)} %param.35) | copy-start | bytes 3076
  7.2 5.0 %copy-start.4 = (f32[16,1024]{1,0:T(8,128)S(1)}, f32[16,1024]{1,0:T(8,128)}, u32[]{:S(2)}) copy-start(f32[16,1024]{1,0:T(8,128)} %param.27) | copy-start | bytes 196612
  7.2 47.8 %all-gather.3.cloned.1.call-start = ((), (), s32[]{:S(2)}) async-start(), calls=%async_computation.4 | async-start | bytes 1327104 | tf_op jit(solution)/shard_map/all_gather | solution.py:61
  7.3 5.1 %copy-start.2 = (bf16[2,64,2,1024]{3,2,1,0:T(2,128)(2,1)S(1)}, bf16[2,64,2,1024]{3,2,1,0:T(2,128)(2,1)}, u32[]{:S(2)}) copy-start(bf16[2,64,2,1024]{3,2,1,0:T(2,128)(2,1)} %param.19) | copy-start | bytes 1572868
  10.5 46.5 %copy-start.8 = (bf16[256,1024]{1,0:T(8,128)(2,1)S(1)}, bf16[256,1024]{1,0:T(8,128)(2,1)}, u32[]{:S(2)}) copy-start(bf16[256,1024]{1,0:T(8,128)(2,1)} %param.25) | copy-start | bytes 1572868
  10.5 46.5 %copy-start.11 = (f32[1024]{0:T(1024)S(1)}, f32[1024]{0:T(1024)}, u32[]{:S(2)}) copy-start(f32[1024]{0:T(1024)} %param.26) | copy-start | bytes 12292
  11.8 244.7 %reduce-scatter.2.cloned.1.call-start = ((), (), s32[]{:S(2)}) async-start(), calls=%async_computation.3 | async-start | bytes 2359296 | tf_op jit(solution)/shard_map/reduce_scatter | solution.py:153
  57.0 8.2 %slice-start.3 = ((s8[8388608]{0:T(1024)(128)(4,1)}), s8[4194304]{0:T(1024)(128)(4,1)S(1)}, s32[]{:S(2)}) async-start(s8[8388608]{0:T(1024)(128)(4,1)} %bitcast.120), calls=%async_computation.8 | async-start | bytes 8388608
  57.7 7.2 %copy-start.7 = (f32[1024]{0:T(1024)S(1)}, f32[1024]{0:T(1024)}, u32[]{:S(2)}) copy-start(f32[1024]{0:T(1024)} %param.28) | copy-start | bytes 12292
  57.7 7.5 %slice-start.4 = ((s8[8388608]{0:T(1024)(128)(4,1)}), s8[4194304]{0:T(1024)(128)(4,1)S(1)}, s32[]{:S(2)}) async-start(s8[8388608]{0:T(1024)(128)(4,1)} %bitcast.120), calls=%async_computation.9 | async-start | bytes 8388608
  65.2 1.3 copy-start.3
  66.5 93.1 %copy-start.9 = (bf16[16,4096]{1,0:T(8,128)(2,1)S(1)}, bf16[16,4096]{1,0:T(8,128)(2,1)}, u32[]{:S(2)}) copy-start(bf16[16,4096]{1,0:T(8,128)(2,1)} %param.31) | copy-start | bytes 393220
  66.5 93.1 %copy-start.10 = (f32[4096]{0:T(1024)S(1)}, f32[4096]{0:T(1024)}, u32[]{:S(2)}) copy-start(f32[4096]{0:T(1024)} %param.30) | copy-start | bytes 49156
  161.7 13.3 %slice-start = ((s8[12582912]{0:T(1024)(128)(4,1)}), s8[4194304]{0:T(1024)(128)(4,1)S(1)}, s32[]{:S(2)}) async-start(s8[12582912]{0:T(1024)(128)(4,1)} %bitcast.118), calls=%async_computation.5 | async-start | bytes 8388608
  168.0 7.0 %slice-start.1 = ((s8[12582912]{0:T(1024)(128)(4,1)}), s8[4194304]{0:T(1024)(128)(4,1)S(1)}, s32[]{:S(2)}) async-start(s8[12582912]{0:T(1024)(128)(4,1)} %bitcast.118), calls=%async_computation.6 | async-start | bytes 8388608
  168.0 7.0 %slice-start.2 = ((s8[12582912]{0:T(1024)(128)(4,1)}), s8[4194304]{0:T(1024)(128)(4,1)S(1)}, s32[]{:S(2)}) async-start(s8[12582912]{0:T(1024)(128)(4,1)} %bitcast.118), calls=%async_computation.7 | async-start | bytes 8388608
  168.0 9.3 %slice-start.5 = ((s8[12582912]{0:T(1024)(128)(4,1)}), s8[4194304]{0:T(1024)(128)(4,1)S(1)}, s32[]{:S(2)}) async-start(s8[12582912]{0:T(1024)(128)(4,1)} %bitcast.122), calls=%async_computation.10 | async-start | bytes 8388608
  168.0 9.4 %slice-start.6 = ((s8[12582912]{0:T(1024)(128)(4,1)}), s8[4194304]{0:T(1024)(128)(4,1)S(1)}, s32[]{:S(2)}) async-start(s8[12582912]{0:T(1024)(128)(4,1)} %bitcast.122), calls=%async_computation.11 | async-start | bytes 8388608
  175.1 3.8 %slice-start.7 = ((s8[12582912]{0:T(1024)(128)(4,1)}), s8[4194304]{0:T(1024)(128)(4,1)S(1)}, s32[]{:S(2)}) async-start(s8[12582912]{0:T(1024)(128)(4,1)} %bitcast.122), calls=%async_computation.12 | async-start | bytes 8388608
  178.9 79.2 %copy-start.1 = (bf16[1024,288]{0,1:T(8,128)(2,1)S(1)}, bf16[1024,288]{0,1:T(8,128)(2,1)}, u32[]{:S(2)}) copy-start(bf16[1024,288]{0,1:T(8,128)(2,1)} %param.24) | copy-start | bytes 1769476
Sparse Core Ops, SparseCore 0:
  11.9 43.0 all-gather.2
  187.9 68.4 reduce-scatter.1
